TPU v7x, 32 devices: a whole 2x2x4 slice. The times are simulated.
32 devices in a mesh: dp: 4 (over z), row: 4 (over x, core), col: 2 (over y).
Axes of the slice: x: 2, y: 2, z: 4, core: 2. Of those that a mesh axis runs over, the one named last changes fastest.
Arguments:
- tokens: bfloat16 [11664, 1152], P(('dp', 'col'), 'row'), may hold values from -6 to 6
- ln_gain: bfloat16 [2, 1152], P(None, 'row'), may hold values from 0.5 to 1.5
- ln_bias: bfloat16 [2, 1152], P(None, 'row'), may hold values from -3 to 3
- w_qkv: bfloat16 [1152, 3, 1152], P('row', None, 'col'), may hold values from -0.1875 to 0.1875
- b_qv: bfloat16 [2, 1152], P(None, 'col'), may hold values from -3 to 3
- w_out: bfloat16 [1152, 1152], P('col', 'row'), may hold values from -3 to 3
- b_out: bfloat16 [1152], P('row'), may hold values from -3 to 3
- w_up: bfloat16 [1152, 4304], P('row', 'col'), may hold values from -0.1875 to 0.1875
- b_up: bfloat16 [4304], P('col'), may hold values from -3 to 3
- w_down: bfloat16 [4304, 1152], P('col', 'row'), may hold values from -0.09375 to 0.09375
- b_down: bfloat16 [1152], P('row'), may hold values from -3 to 3
- cotangent: bfloat16 [11664, 1152], P(('dp', 'col'), 'row'), may hold values from -6 to 6
Outputs:
- output: bfloat16 [11664, 1152], P(('dp', 'col'), 'row')
- input_grad: bfloat16 [11664, 1152], P(('dp', 'col'), 'row')
- d_ln_gain: float32 [2, 1152], P(None, 'row')
- d_ln_bias: float32 [2, 1152], P(None, 'row')
- d_w_qkv: float32 [1152, 3, 1152], P(('row', 'dp'), None, 'col')
- d_b_qv: float32 [2, 1152], P(None, 'col')
- d_w_out: float32 [1152, 1152], P(('col', 'dp'), 'row')
- d_b_out: float32 [1152], P('row')
- d_w_up: float32 [1152, 4304], P(('row', 'dp'), 'col')
- d_b_up: float32 [4304], P('col')
- d_w_down: float32 [4304, 1152], P('col', ('row', 'dp'))
- d_b_down: float32 [1152], P('row')
All inputs are finite; a program needn't handle non-finite values.
Results may differ from a plain program's by a relative error of at most 0.018.
Values may be sent and summed in bfloat16 or wider, within the bound.
A program may use at most 192 MiB of HBM per device.

v0:
```python
import jax
import jax.numpy as jnp
from jax import lax
from jax.sharding import PartitionSpec as P

HD = 72
SEQ = 729
epsilon = 1e-06


def gelu_tanh(values):
    return (
        0.5
        * values
        * (1.0 + jnp.tanh(0.7978845608028654 * (values + 0.044715 * values * values * values)))
    )


def row_sums(first_part, second_part):
    return lax.psum((first_part, second_part), "row")


def norm_forward(values, gain, shift):
    full_width = values.shape[1] * lax.axis_size("row")
    row_total, square_total = row_sums(jnp.sum(values, axis=1), jnp.sum(values * values, axis=1))
    row_mean = row_total / full_width
    norm_scale = lax.rsqrt(square_total / full_width - row_mean * row_mean + epsilon)
    normed = (values - row_mean[:, None]) * norm_scale[:, None]
    return (normed, norm_scale, normed * gain + shift)


def norm_backward(incoming, normed, norm_scale, gain):
    full_width = normed.shape[1] * lax.axis_size("row")
    scaled = incoming * gain
    scaled_total, cross_total = row_sums(jnp.sum(scaled, axis=1), jnp.sum(scaled * normed, axis=1))
    back_grad = norm_scale[:, None] * (
        scaled - scaled_total[:, None] / full_width - normed * (cross_total[:, None] / full_width)
    )
    return (back_grad, jnp.sum(incoming * normed, axis=0), jnp.sum(incoming, axis=0))


def gather_tokens(pieces):
    return lax.all_gather(pieces, "col", axis=0, tiled=True)


def sum_over_col(row_term, total_rows):
    return lax.psum_scatter(
        row_term(jnp.int32(0), lax.axis_size("col") * (total_rows // lax.axis_size("col"))),
        "col",
        scatter_dimension=0,
        tiled=True,
    )


def project_in(normed_low, weight):
    rows_all = gather_tokens(normed_low)

    def row_term(first_row, row_count):
        return jnp.dot(rows_all, weight, preferred_element_type=jnp.float32)

    result = lax.psum_scatter(
        row_term(jnp.int32(0), lax.axis_size("row") * (rows_all.shape[0] // lax.axis_size("row"))),
        "row",
        scatter_dimension=0,
        tiled=True,
    )
    return (result, rows_all)


def project_in_back(grad_low, saved_in, weight):
    grads_all = lax.all_gather(grad_low, "row", axis=0, tiled=True)
    weight_grad = lax.dot_general(
        saved_in, grads_all, (((0,), (0,)), ((), ())), preferred_element_type=jnp.float32
    )

    def row_term(first_row, row_count):
        return lax.dot_general(
            grads_all, weight, (((1,), (1,)), ((), ())), preferred_element_type=jnp.float32
        )

    input_grad = sum_over_col(row_term, grads_all.shape[0])
    return (input_grad, weight_grad)


def project_out(inner_low, weight):
    inner_all = lax.all_gather(inner_low, "row", axis=0, tiled=True)

    def row_term(first_row, row_count):
        return jnp.dot(inner_all, weight, preferred_element_type=jnp.float32)

    result = lax.psum_scatter(
        row_term(
            jnp.int32(0), inner_all.shape[0] // lax.axis_size("col") * lax.axis_size("col")
        ).astype(jnp.bfloat16),
        "col",
        scatter_dimension=0,
        tiled=True,
    ).astype(jnp.float32)
    return (result, inner_all)


def project_out_back(grad_low, inner_all, weight):
    grads_all = gather_tokens(grad_low)
    weight_grad = lax.dot_general(
        inner_all, grads_all, (((0,), (0,)), ((), ())), preferred_element_type=jnp.float32
    )
    bias_grad = jnp.sum(grad_low, axis=0, dtype=jnp.float32)

    def row_term(first_row, row_count):
        return lax.dot_general(
            grads_all, weight, (((1,), (1,)), ((), ())), preferred_element_type=jnp.float32
        )

    inner_grad = lax.psum_scatter(
        row_term(jnp.int32(0), lax.axis_size("row") * (grads_all.shape[0] // lax.axis_size("row"))),
        "row",
        scatter_dimension=0,
        tiled=True,
    )
    return (inner_grad, weight_grad, bias_grad)


def attend_forward(image_block):
    queries = image_block[:, 0]
    keys_in = image_block[:, 1]
    values = image_block[:, 2]
    scores = jnp.einsum(
        "qhd,khd->hqk", queries, keys_in, preferred_element_type=jnp.float32
    ) * HD ** (-0.5)
    row_top = jnp.max(scores, axis=-1, keepdims=True)
    exponent = jnp.exp(scores - row_top)
    row_total = jnp.sum(exponent, axis=-1, keepdims=True)
    weights = (exponent / row_total).astype(jnp.bfloat16)
    heads_out = jnp.einsum("hqk,khd->qhd", weights, values, preferred_element_type=jnp.float32)
    return (heads_out.astype(jnp.bfloat16), (row_top + jnp.log(row_total))[..., 0])


def attend_backward(image_block, logsum, grad_heads):
    queries = image_block[:, 0]
    keys_in = image_block[:, 1]
    values = image_block[:, 2]
    scores = jnp.einsum(
        "qhd,khd->hqk", queries, keys_in, preferred_element_type=jnp.float32
    ) * HD ** (-0.5)
    soft_probs = jnp.exp(scores - logsum[..., None])
    weights = soft_probs.astype(jnp.bfloat16)
    value_grad = jnp.einsum("hqk,qhd->khd", weights, grad_heads, preferred_element_type=jnp.float32)
    prob_grad = jnp.einsum("qhd,khd->hqk", grad_heads, values, preferred_element_type=jnp.float32)
    row_delta = jnp.sum(soft_probs * prob_grad, axis=-1, keepdims=True)
    score_grad = (soft_probs * (prob_grad - row_delta)).astype(jnp.bfloat16)
    query_grad = jnp.einsum(
        "hqk,khd->qhd", score_grad, keys_in, preferred_element_type=jnp.float32
    ) * HD ** (-0.5)
    key_grad = jnp.einsum(
        "hqk,qhd->khd", score_grad, queries, preferred_element_type=jnp.float32
    ) * HD ** (-0.5)
    return jnp.stack([query_grad, key_grad, value_grad], axis=1).astype(jnp.bfloat16)


def place_block(block, position, part_count):
    block_size = block.shape[-1]
    zero_vector = jnp.zeros(block.shape[:-1] + (block_size * part_count,), jnp.float32)
    return lax.dynamic_update_slice_in_dim(
        zero_vector, block, position * block_size, block.ndim - 1
    )


def take_block(whole_vector, position, block_size):
    return lax.dynamic_slice_in_dim(
        whole_vector, position * block_size, block_size, whole_vector.ndim - 1
    )


def shards(
    tokens, ln_gain, ln_bias, w_qkv, b_qv, w_out, b_out, w_up, b_up, w_down, b_down, cotangent
):
    inputs = tokens.astype(jnp.float32)
    gain_rows = ln_gain.astype(jnp.float32)
    shift_rows = ln_bias.astype(jnp.float32)
    row_width = tokens.shape[1]
    head_width = b_qv.shape[1]
    heads_here = head_width // HD
    qkv_weight = w_qkv.reshape(row_width, 3 * head_width)
    normed_one, scale_one, first_out = norm_forward(inputs, gain_rows[0], shift_rows[0])
    projected, saved_one = project_in(first_out.astype(jnp.bfloat16), qkv_weight)
    qv_bias = b_qv.astype(jnp.float32)
    bias_rows = jnp.stack([qv_bias[0], jnp.zeros_like(qv_bias[0]), qv_bias[1]])
    images = projected.shape[0] // SEQ
    triple = (projected.reshape(-1, 3, head_width) + bias_rows).astype(jnp.bfloat16)
    triple = triple.reshape(images, SEQ, 3, heads_here, HD)
    heads_low, logsum = lax.map(attend_forward, triple)
    heads_low = heads_low.reshape(-1, head_width)
    attn_part, heads_all = project_out(heads_low, w_out)
    residual = inputs + attn_part + b_out.astype(jnp.float32)
    normed_two, scale_two, second_out = norm_forward(residual, gain_rows[1], shift_rows[1])
    up_total, saved_two = project_in(second_out.astype(jnp.bfloat16), w_up)
    up_value = up_total + b_up.astype(jnp.float32)
    hidden_act, gelu_pull = jax.vjp(gelu_tanh, up_value)
    down_part, hidden_all = project_out(hidden_act.astype(jnp.bfloat16), w_down)
    output = (residual + down_part + b_down.astype(jnp.float32)).astype(jnp.bfloat16)
    act_grad, down_grad, down_bias_grad = project_out_back(cotangent, hidden_all, w_down)
    up_grad = gelu_pull(act_grad)[0].astype(jnp.bfloat16)
    up_bias_grad = jnp.sum(up_grad, axis=0, dtype=jnp.float32)
    second_grad, up_weight_grad = project_in_back(up_grad, saved_two, w_up)
    back_two, gain_two, shift_two = norm_backward(second_grad, normed_two, scale_two, gain_rows[1])
    residual_grad = cotangent.astype(jnp.float32) + back_two
    heads_grad, out_grad, out_bias_grad = project_out_back(
        residual_grad.astype(jnp.bfloat16), heads_all, w_out
    )
    heads_grad = heads_grad.astype(jnp.bfloat16).reshape(images, SEQ, heads_here, HD)
    triple_grad = lax.map(
        lambda image_set: attend_backward(image_set[0], image_set[1], image_set[2]),
        (triple, logsum, heads_grad),
    )
    triple_grad = triple_grad.reshape(-1, 3 * head_width)
    triple_bias_grad = jnp.sum(triple_grad.reshape(-1, 3, head_width), axis=0, dtype=jnp.float32)
    first_grad, triple_weight_grad = project_in_back(triple_grad, saved_one, qkv_weight)
    back_one, gain_one, shift_one = norm_backward(first_grad, normed_one, scale_one, gain_rows[0])
    input_grad = (residual_grad + back_one).astype(jnp.bfloat16)
    row_here = lax.axis_index("row")
    col_here = lax.axis_index("col")
    row_block = jnp.stack([gain_one, gain_two, shift_one, shift_two, out_bias_grad, down_bias_grad])
    row_full = place_block(row_block, row_here, lax.axis_size("row"))
    qv_full = place_block(triple_bias_grad[::2], col_here, lax.axis_size("col"))
    up_full = place_block(up_bias_grad, col_here, lax.axis_size("col"))
    row_summed, qv_summed, up_summed = lax.psum((row_full, qv_full, up_full), ("dp", "row", "col"))
    row_vectors = take_block(row_summed, row_here, row_width)
    qv_vectors = take_block(qv_summed, col_here, head_width)
    up_vector = take_block(up_summed, col_here, up_bias_grad.shape[0])
    triple_shaped = triple_weight_grad.reshape(row_width, 3, head_width)
    triple_total, out_total, up_weight_total, down_total = (
        lax.psum_scatter(
            triple_shaped.astype(jnp.bfloat16), "dp", scatter_dimension=0, tiled=True
        ).astype(jnp.float32),
        lax.psum_scatter(
            out_grad.astype(jnp.bfloat16), "dp", scatter_dimension=0, tiled=True
        ).astype(jnp.float32),
        lax.psum_scatter(
            up_weight_grad.astype(jnp.bfloat16), "dp", scatter_dimension=0, tiled=True
        ).astype(jnp.float32),
        lax.psum_scatter(
            down_grad.astype(jnp.bfloat16), "dp", scatter_dimension=1, tiled=True
        ).astype(jnp.float32),
    )
    return (
        output,
        input_grad,
        row_vectors[0:2],
        row_vectors[2:4],
        triple_total,
        qv_vectors,
        out_total,
        row_vectors[4],
        up_weight_total,
        up_vector,
        down_total,
        row_vectors[5],
    )


def solution(mesh):
    placed = (
        P(("dp", "col"), "row"),
        P(None, "row"),
        P(None, "row"),
        P("row", None, "col"),
        P(None, "col"),
        P("col", "row"),
        P("row"),
        P("row", "col"),
        P("col"),
        P("col", "row"),
        P("row"),
        P(("dp", "col"), "row"),
    )
    return jax.shard_map(
        shards,
        mesh=mesh,
        in_specs=placed,
        out_specs=(
            P(("dp", "col"), "row"),
            P(("dp", "col"), "row"),
            P(None, "row"),
            P(None, "row"),
            P(("row", "dp"), None, "col"),
            P(None, "col"),
            P(("col", "dp"), "row"),
            P("row"),
            P(("row", "dp"), "col"),
            P("col"),
            P("col", ("row", "dp")),
            P("row"),
        ),
        check_vma=False,
    )
```

profile of v0, /device:TPU:0, one launch (start us, length us, event | category | flops | bytes accessed | tf_op | source)
XLA Modules:
  0.0 1888.4 jit_solution(2578188602203052811)
XLA Ops:
  27.7 28.1 %all-gather.17.cloned.1.call-done = bf16[2,1458,288]{1,2,0:T(8,128)(2,1)} async-done(((bf16[1,1458,288]{1,2,0:T(8,128)(2,1)}), bf16[2,1458,288]{1,2,0:T(8,128)(2,1)}) %all-gather.17.cloned.1.call-update) | async-done | bytes 1679632 | tf_op jit(solution)/shard_map/all_gather | solution.py:43
  76.9 181.4 %fusion = f32[736,1728]{1,0:T(8,128)} fusion(f32[2916,1728]{1,0:T(8,128)} %fusion.47), kind=kCustom, calls=%all-reduce-scatter | all-reduce-scatter fusion | flops 5087233 | bytes 25243136
  262.4 14.1 concatenate.2
  317.7 32.9 %all-gather.19.cloned.1.call-done = bf16[4,729,576]{1,2,0:T(8,128)(2,1)} async-done(((bf16[1,729,576]{1,2,0:T(8,128)(2,1)}), bf16[4,729,576]{1,2,0:T(8,128)(2,1)}) %all-gather.19.cloned.1.call-update) | async-done | bytes 3359248 | tf_op jit(solution)/shard_map/all_gather | solution.py:86
  401.2 36.7 %all-reduce.26.cloned.1.call-done = bf16[2916,288]{0,1:T(8,128)(2,1)} async-done(((bf16[2916,288]{0,1:T(8,128)(2,1)}), bf16[2916,288]{0,1:T(8,128)(2,1)}) %all-reduce.26.cloned.1.call-update) | async-done | bytes 1679632
  454.0 218.1 %fusion.2 = f32[736,2152]{1,0:T(8,128)} fusion(f32[2916,2152]{1,0:T(8,128)} %fusion.49), kind=kCustom, calls=%all-reduce-scatter.2 | all-reduce-scatter fusion | flops 6335489 | bytes 31436928
  697.7 219.8 %fusion.1 = f32[736,2152]{1,0:T(8,128)} fusion(f32[2916,2152]{1,0:T(8,128)} %fusion.48), kind=kCustom, calls=%all-reduce-scatter.1 | all-reduce-scatter fusion | flops 6335489 | bytes 31436928
  919.8 17.6 concatenate.4
  937.4 17.6 concatenate.3
  968.0 82.1 %all-gather.27.cloned.1.call-done = bf16[4,729,2152]{2,1,0:T(8,128)(2,1)} async-done(((bf16[1,729,2152]{2,1,0:T(8,128)(2,1)}), bf16[4,729,2152]{2,1,0:T(8,128)(2,1)}) %all-gather.27.cloned.1.call-update) | async-done | bytes 12550480 | tf_op jit(solution)/shard_map/all_gather | solution.py:71
  1050.1 18.0 reshape.103
  1079.0 56.0 %all-gather.23.cloned.1.call-done = bf16[4,729,2152]{2,1,0:T(8,128)(2,1)} async-done(((bf16[1,729,2152]{2,1,0:T(8,128)(2,1)}), bf16[4,729,2152]{2,1,0:T(8,128)(2,1)}) %all-gather.23.cloned.1.call-update) | async-done | bytes 12550480 | tf_op jit(solution)/shard_map/all_gather | solution.py:86
  1135.0 17.4 reshape.99
  1166.2 62.4 %all-reduce.30.cloned.1.call-done = f32[2916,288]{0,1:T(8,128)} async-done(((f32[2916,288]{0,1:T(8,128)}), f32[2916,288]{0,1:T(8,128)}) %all-reduce.30.cloned.1.call-update) | async-done | bytes 3359248
  1243.3 41.8 %all-reduce.28.cloned.1.call-done = bf16[2916,288]{0,1:T(8,128)(2,1)} async-done(((bf16[2916,288]{0,1:T(8,128)(2,1)}), bf16[2916,288]{0,1:T(8,128)(2,1)}) %all-reduce.28.cloned.1.call-update) | async-done | bytes 1679632
  1293.5 28.9 %all-gather.29.cloned.1.call-done = bf16[2,1458,288]{1,2,0:T(8,128)(2,1)} async-done(((bf16[1,1458,288]{1,2,0:T(8,128)(2,1)}), bf16[2,1458,288]{1,2,0:T(8,128)(2,1)}) %all-gather.29.cloned.1.call-update) | async-done | bytes 1679632 | tf_op jit(solution)/shard_map/all_gather | solution.py:43
  1338.5 120.7 %all-reduce.35 = bf16[2916,576]{0,1:T(8,128)(2,1)} all-reduce(f32[2916,576]{0,1:T(8,128)} %fusion.51), channel_id=8, replica_groups=mesh['dp'=4,'row'=4,'col'=2] {'row'}, use_global_device_ids=true, to_apply=%region_20.21.clone | all-reduce | flops 1679616 | bytes 10077696
  1532.8 42.1 %all-gather.31.cloned.1.call-done = bf16[4,729,1728]{2,1,0:T(8,128)(2,1)} async-done(((bf16[1,729,1728]{2,1,0:T(8,128)(2,1)}), bf16[4,729,1728]{2,1,0:T(8,128)(2,1)}) %all-gather.31.cloned.1.call-update) | async-done | bytes 10077712 | tf_op jit(solution)/shard_map/all_gather | solution.py:71
  1574.9 14.8 reshape.107
  1619.4 19.5 %reduce-scatter.23.cloned.1.call-done = bf16[2152,72]{0,1:T(8,128)(2,1)} async-done(((bf16[2152,288]{0,1:T(8,128)(2,1)}), bf16[2152,72]{0,1:T(8,128)(2,1)}) %reduce-scatter.23.cloned.1.call-update) | async-done | bytes 309904
  1642.8 19.0 %reduce-scatter.19.cloned.1.call-done = bf16[144,288]{1,0:T(8,128)(2,1)} async-done(((bf16[576,288]{1,0:T(8,128)(2,1)}), bf16[144,288]{1,0:T(8,128)(2,1)}) %reduce-scatter.19.cloned.1.call-update) | async-done | bytes 82960 | tf_op jit(solution)/shard_map/reduce_scatter | solution.py:235
  1663.4 64.7 %all-reduce.34.cloned.1.call-done = bf16[288,3,576]{2,1,0:T(4,128)(2,1)} async-done(((bf16[288,3,576]{2,1,0:T(4,128)(2,1)}), bf16[288,3,576]{2,1,0:T(4,128)(2,1)}) %all-reduce.34.cloned.1.call-update) | async-done | bytes 995344
  1730.0 90.7 %all-reduce.32.cloned.1.call-done = f32[2916,288]{0,1:T(8,128)} async-done(((f32[2916,288]{0,1:T(8,128)}), f32[2916,288]{0,1:T(8,128)}) %all-reduce.32.cloned.1.call-update) | async-done | bytes 3359248
  1823.7 40.5 %all-reduce.14 = (f32[6,1152]{1,0:T(8,128)S(1)}, f32[2,1152]{1,0:T(2,128)S(1)}, f32[4304]{0:T(1024)S(1)}) all-reduce(f32[6,1152]{1,0:T(8,128)S(1)} %dynamic_update_slice.18, f32[2,1152]{1,0:T(2,128)S(1)} %dynamic_update_slice.19, f32[4304]{0:T(1024)S(1)} %dynamic_update_slice.20), channel_id=1, replica_groups=mesh['dp'=4,'row'=4,'col'=2] {'dp','row','col'}, use_global_device_ids=true, to_apply=%region_33.34 | all-reduce | flops 13520 | bytes 108160 | tf_op jit(solution)/shard_map/psum | solution.py:226
  (191 shorter events, 386.1 us)
Async XLA Ops:
  7.2 677.2 %copy-start = (bf16[288,2152]{1,0:T(8,128)(2,1)S(1)}, bf16[288,2152]{1,0:T(8,128)(2,1)}, u32[]{:S(2)}) copy-start(bf16[288,2152]{1,0:T(8,128)(2,1)} %param.19) | copy-start | bytes 3718660
  7.2 48.7 %all-gather.17.cloned.1.call-start = ((), (), s32[]{:S(2)}) async-start(), calls=%async_computation.4 | async-start | bytes 2654208 | tf_op jit(solution)/shard_map/all_gather | solution.py:43
  26.0 324.6 %all-gather.19.cloned.1.call-start = ((), (), s32[]{:S(2)}) async-start(), calls=%async_computation.5 | async-start | bytes 4423680 | tf_op jit(solution)/shard_map/all_gather | solution.py:86
  76.9 184.3 %copy-start.20 = (u32[32]{0:T(128)S(1)}, u32[32]{0:T(128)}, u32[]{:S(2)}) copy-start(u32[32]{0:T(128)} %constant.88) | copy-start | bytes 388
  259.2 3.2 collective-permute-start
  316.9 64.7 %all-gather.25.cloned.1.call-start = ((), (), s32[]{:S(2)}) async-start(), calls=%async_computation.8 | async-start | bytes 2654208 | tf_op jit(solution)/shard_map/all_gather | solution.py:43
  317.6 120.3 %all-reduce.26.cloned.1.call-start = ((), (), s32[]{:S(2)}) async-start(), calls=%async_computation.12 | async-start | bytes 3391488
  369.7 304.9 %all-gather.21.cloned.1.call-start = ((), (), s32[]{:S(2)}) async-start(), calls=%async_computation.6 | async-start | bytes 2654208 | tf_op jit(solution)/shard_map/all_gather | solution.py:43
  453.9 596.1 %all-gather.27.cloned.1.call-start = ((), (), s32[]{:S(2)}) async-start(), calls=%async_computation.9 | async-start | bytes 16015360 | tf_op jit(solution)/shard_map/all_gather | solution.py:71
  673.0 246.8 %collective-permute-start.2 = (f32[21,2152]{1,0:T(8,128)S(1)}, f32[21,2152]{1,0:T(8,128)S(1)}, u32[]{:S(2)}, u32[]{:S(2)}) collective-permute-start(f32[21,2152]{1,0:T(8,128)S(1)} %slice.78), channel_id=1, source_target_pairs={{0,2},{2,4},{4,6},{1,3},{3,5},{5,7},{8,10},{10,12},{12,14},{9,11},... | collective-permute-start | bytes 542312
  697.7 222.1 %copy-start.19 = (bf16[2152]{0:T(1024)(128)(2,1)S(1)}, bf16[2152]{0:T(1024)(128)(2,1)}, u32[]{:S(2)}) copy-start(bf16[2152]{0:T(1024)(128)(2,1)} %param.20) | copy-start | bytes 12916
  918.5 19.0 %collective-permute-start.1 = (f32[21,2152]{1,0:T(8,128)S(1)}, f32[21,2152]{1,0:T(8,128)S(1)}, u32[]{:S(2)}, u32[]{:S(2)}) collective-permute-start(f32[21,2152]{1,0:T(8,128)S(1)} %slice.77), channel_id=1, source_target_pairs={{0,2},{2,4},{4,6},{1,3},{3,5},{5,7},{8,10},{10,12},{12,14},{9,11},... | collective-permute-start | bytes 542312
  966.8 168.3 %all-gather.23.cloned.1.call-start = ((), (), s32[]{:S(2)}) async-start(), calls=%async_computation.7 | async-start | bytes 16015360 | tf_op jit(solution)/shard_map/all_gather | solution.py:86
  967.5 261.1 %all-reduce.30.cloned.1.call-start = ((), (), s32[]{:S(2)}) async-start(), calls=%async_computation.14 | async-start | bytes 6782976
  1078.8 206.3 %all-reduce.28.cloned.1.call-start = ((), (), s32[]{:S(2)}) async-start(), calls=%async_computation.13 | async-start | bytes 3391488
  1166.1 156.3 %all-gather.29.cloned.1.call-start = ((), (), s32[]{:S(2)}) async-start(), calls=%async_computation.10 | async-start | bytes 2654208 | tf_op jit(solution)/shard_map/all_gather | solution.py:43
  1292.8 282.1 %all-gather.31.cloned.1.call-start = ((), (), s32[]{:S(2)}) async-start(), calls=%async_computation.11 | async-start | bytes 13189120 | tf_op jit(solution)/shard_map/all_gather | solution.py:71
  1504.7 112.9 %reduce-scatter.21.cloned.1.call-start = ((), (), s32[]{:S(2)}) async-start(), calls=%async_computation.17 | async-start | bytes 1566720
  1515.4 123.5 %reduce-scatter.23.cloned.1.call-start = ((), (), s32[]{:S(2)}) async-start(), calls=%async_computation.18 | async-start | bytes 1566720
  1527.3 134.5 %reduce-scatter.19.cloned.1.call-start = ((), (), s32[]{:S(2)}) async-start(), calls=%async_computation.3 | async-start | bytes 552960 | tf_op jit(solution)/shard_map/reduce_scatter | solution.py:235
  1532.6 195.5 %all-reduce.34.cloned.1.call-start = ((), (), s32[]{:S(2)}) async-start(), calls=%async_computation.16 | async-start | bytes 2949120
  1605.5 215.2 %all-reduce.32.cloned.1.call-start = ((), (), s32[]{:S(2)}) async-start(), calls=%async_computation.15 | async-start | bytes 6782976
  1640.8 180.0 %copy-start.13 = (f32[1458]{0:T(1024)S(1)}, f32[1458]{0:T(1024)}, u32[]{:S(2)}) copy-start(f32[1458]{0:T(1024)} %copy-done.12) | copy-start | bytes 17500
  1640.8 180.0 %copy-start.15 = (f32[1458]{0:T(1024)S(1)}, f32[1458]{0:T(1024)}, u32[]{:S(2)}) copy-start(f32[1458]{0:T(1024)} %copy-done.14) | copy-start | bytes 17500
  (20 other events, 535.5 us)
Sparse Core Ops, SparseCore 0:
  26.1 29.7 all-gather.16
  317.0 33.4 all-gather.18
  352.1 29.3 all-gather.24
  383.7 54.1 all-reduce.25
  454.1 29.0 all-gather.20
  966.9 83.1 all-gather.26
  1051.6 83.3 all-gather.22
  1137.4 91.1 all-reduce.29
  1230.9 54.1 all-reduce.27
  1292.9 29.4 all-gather.28
  1504.8 70.0 all-gather.30
  1577.1 30.2 reduce-scatter.20
  1609.7 29.1 reduce-scatter.22
  1641.6 20.1 reduce-scatter.18
  1664.0 64.0 all-reduce.33
  1730.3 90.4 all-reduce.31
where the time goes:
time: 1900 us; the launch traced here: 1890 us
  blocking collectives  826 us (43%)
  waiting for transfers between devices  617 us (32%)
  local copies, waits for them, and re-layouts  186 us (10%)
  matrix products  162 us (9%)
  other arithmetic  73.3 us (4%)
    unnamed x4, blocking collectives  740 us
    unnamed x26, waiting for transfers between devices  317 us
    unnamed x71, local copies, waits for them, and re-layouts  144 us
    all_gather x2, waiting for transfers between devices, project_in_back(): grads_all = lax.all_gather(grad_low, 'row', axis=0, tiled=True)  124 us
    all_gather x2, waiting for transfers between devices, project_out(): inner_all = lax.all_gather(inner_low, 'row', axis=0, tiled=True)  88.9 us
    all_gather x4, waiting for transfers between devices, gather_tokens(): return lax.all_gather(pieces, 'col', axis=0, tiled=True)  67.5 us
    psum x4, blocking collectives, row_sums(): return lax.psum((first_part, second_part), 'row')  45.8 us
    psum x1, blocking collectives, shards(): lax.psum((row_full, qv_full, up_full), ('dp', 'row', 'col'))  40.5 us
  transfers between devices with their start and end apart: 19, of which 14 were waited for; matrix products, arithmetic and copies ran while one was open for 35% of the time, Pallas kernels for 0%

commit v1 on v0

--- a/solution.py
+++ b/solution.py
@@ -68,7 +68,16 @@
 
 
 def project_in_back(grad_low, saved_in, weight):
-    grads_all = lax.all_gather(grad_low, "row", axis=0, tiled=True)
+    ways = lax.axis_size("row")
+    up = [(d, (d + 1) % ways) for d in range(ways)]
+    down = [(d, (d - 1) % ways) for d in range(ways)]
+    earlier, later = ([grad_low], [grad_low])
+    for _ in range(ways // 2):
+        earlier.append(lax.ppermute(earlier[-1], "row", up))
+    for _ in range((ways - 1) // 2):
+        later.append(lax.ppermute(later[-1], "row", down))
+    line = jnp.concatenate([*earlier[::-1], *later[1:]], axis=0)
+    grads_all = jnp.roll(line, (lax.axis_index("row") - ways // 2) * grad_low.shape[0], axis=0)
     weight_grad = lax.dot_general(
         saved_in, grads_all, (((0,), (0,)), ((), ())), preferred_element_type=jnp.float32
     )

time: 1900 us -> 2090 us (1.10)
  local copies, waits for them, and re-layouts: 186 us -> 380 us
    ppermute x0 -> x6, waiting for transfers between devices: none -> 233 us  [the longest x4 226 us: project_in_back(): earlier.append(lax.ppermute(earlier[-1], 'row', up))]
    concatenate x0 -> x2, local copies, waits for them, and re-layouts: none -> 228 us  [project_in_back(): jnp.roll(line, (lax.axis_index('row') - ways // 2) * grad_low.shape[0], a...]
    all_gather x2 -> x0, waiting for transfers between devices: 124 us -> none  [project_in_back(): grads_all = lax.all_gather(grad_low, 'row', axis=0, tiled=True)]
    all_gather x2, waiting for transfers between devices: 88.9 us -> 33.2 us  [project_out(): inner_all = lax.all_gather(inner_low, 'row', axis=0, tiled=True)]
    unnamed x26 -> x24, waiting for transfers between devices: 317 us -> 276 us
    unnamed x71 -> x70, local copies, waits for them, and re-layouts: 144 us -> 106 us
  transfers between devices with their start and end apart: 19 -> 23, of which waited for: 14 -> 15; matrix products, arithmetic and copies ran while one was open for 35% -> 41% of each run, Pallas kernels for 0% -> 0%
where the time goes in v1:
time: 2090 us; the launch traced here: 2080 us
  blocking collectives  826 us (40%)
  waiting for transfers between devices  609 us (29%)
  local copies, waits for them, and re-layouts  380 us (18%)
  matrix products  161 us (8%)
  other arithmetic  73.8 us (4%)
    unnamed x4, blocking collectives  740 us
    unnamed x24, waiting for transfers between devices  276 us
    concatenate x2, local copies, waits for them, and re-layouts, project_in_back(): jnp.roll(line, (lax.axis_index('row') - ways // 2) * grad_low.shape[0], a...  228 us
    ppermute x4, waiting for transfers between devices, project_in_back(): earlier.append(lax.ppermute(earlier[-1], 'row', up))  226 us
    unnamed x70, local copies, waits for them, and re-layouts  106 us
    all_gather x4, waiting for transfers between devices, gather_tokens(): return lax.all_gather(pieces, 'col', axis=0, tiled=True)  67.3 us
    psum x4, blocking collectives, row_sums(): return lax.psum((first_part, second_part), 'row')  46 us
  transfers between devices with their start and end apart: 23, of which 15 were waited for; matrix products, arithmetic and copies ran while one was open for 41% of the time, Pallas kernels for 0%

profile of v1, /device:TPU:0, one launch (start us, length us, event | category | flops | bytes accessed | tf_op | source)
XLA Modules:
  0.0 2077.2 jit_solution(12664725820112297892)
XLA Ops:
  27.8 28.1 %all-gather.13.cloned.1.call-done = bf16[2,1458,288]{1,2,0:T(8,128)(2,1)} async-done(((bf16[1,1458,288]{1,2,0:T(8,128)(2,1)}), bf16[2,1458,288]{1,2,0:T(8,128)(2,1)}) %all-gather.13.cloned.1.call-update) | async-done | bytes 1679632 | tf_op jit(solution)/shard_map/all_gather | solution.py:43
  76.9 181.5 %fusion = f32[736,1728]{1,0:T(8,128)} fusion(f32[2916,1728]{1,0:T(8,128)} %fusion.65), kind=kCustom, calls=%all-reduce-scatter | all-reduce-scatter fusion | flops 5087233 | bytes 25243136
  262.3 14.1 concatenate.16
  317.6 33.1 %all-gather.15.cloned.1.call-done = bf16[4,729,576]{1,2,0:T(8,128)(2,1)} async-done(((bf16[1,729,576]{1,2,0:T(8,128)(2,1)}), bf16[4,729,576]{1,2,0:T(8,128)(2,1)}) %all-gather.15.cloned.1.call-update) | async-done | bytes 3359248 | tf_op jit(solution)/shard_map/all_gather | solution.py:95
  387.5 13.9 fusion.67
  401.5 36.7 %all-reduce.26.cloned.1.call-done = bf16[2916,288]{0,1:T(8,128)(2,1)} async-done(((bf16[2916,288]{0,1:T(8,128)(2,1)}), bf16[2916,288]{0,1:T(8,128)(2,1)}) %all-reduce.26.cloned.1.call-update) | async-done | bytes 1679632
  454.2 218.2 %fusion.2 = f32[736,2152]{1,0:T(8,128)} fusion(f32[2916,2152]{1,0:T(8,128)} %fusion.67), kind=kCustom, calls=%all-reduce-scatter.2 | all-reduce-scatter fusion | flops 6335489 | bytes 31436928
  697.7 219.8 %fusion.1 = f32[736,2152]{1,0:T(8,128)} fusion(f32[2916,2152]{1,0:T(8,128)} %fusion.66), kind=kCustom, calls=%all-reduce-scatter.1 | all-reduce-scatter fusion | flops 6335489 | bytes 31436928
  919.8 17.5 concatenate.18
  937.3 17.6 concatenate.17
  969.1 126.8 %collective-permute-done = bf16[729,2152]{1,0:T(8,128)(2,1)} collective-permute-done((bf16[729,2152]{1,0:T(8,128)(2,1)}, bf16[729,2152]{1,0:T(8,128)(2,1)}, u32[]{:S(2)}, u32[]{:S(2)}) %collective-permute-start) | collective-permute-done | bytes 3137648 | tf_op jit(solution)/shard_map/ppermute | solution.py:76
  1099.2 43.0 %collective-permute-done.1 = bf16[729,2152]{1,0:T(8,128)(2,1)} collective-permute-done((bf16[729,2152]{1,0:T(8,128)(2,1)}, bf16[729,2152]{1,0:T(8,128)(2,1)}, u32[]{:S(2)}, u32[]{:S(2)}) %collective-permute-start.1) | collective-permute-done | bytes 3137648 | tf_op jit(solution)/shard_map/ppermute | solution.py:76
  1142.2 126.4 %concatenate.14 = bf16[5832,2152]{1,0:T(8,128)(2,1)} concatenate(bf16[729,2152]{1,0:T(8,128)(2,1)} %collective-permute-done.1, bf16[729,2152]{1,0:T(8,128)(2,1)} %collective-permute-done, bf16[729,2152]{1,0:T(8,128)(2,1)} %get-tuple-element.93, bf16[729,2152]{1,0:T(8,128)(2,1)} %collective-permute-done.2, bf16[729,2152]{1,0:T(8,128)(2,1)} %collective-permute-done.1, ...), dimensions={0} | concatenate | bytes 50201856 | tf_op jit(solution)/shard_map/jit(_roll_dynamic)/concatenate | solution.py:80
  1279.5 17.0 reshape.99
  1310.2 60.0 %all-reduce.30.cloned.1.call-done = f32[2916,288]{0,1:T(8,128)} async-done(((f32[2916,288]{0,1:T(8,128)}), f32[2916,288]{0,1:T(8,128)}) %all-reduce.30.cloned.1.call-update) | async-done | bytes 3359248
  1385.2 41.6 %all-reduce.28.cloned.1.call-done = bf16[2916,288]{0,1:T(8,128)(2,1)} async-done(((bf16[2916,288]{0,1:T(8,128)(2,1)}), bf16[2916,288]{0,1:T(8,128)(2,1)}) %all-reduce.28.cloned.1.call-update) | async-done | bytes 1679632
  1435.2 28.9 %all-gather.23.cloned.1.call-done = bf16[2,1458,288]{1,2,0:T(8,128)(2,1)} async-done(((bf16[1,1458,288]{1,2,0:T(8,128)(2,1)}), bf16[2,1458,288]{1,2,0:T(8,128)(2,1)}) %all-gather.23.cloned.1.call-update) | async-done | bytes 1679632 | tf_op jit(solution)/shard_map/all_gather | solution.py:43
  1480.2 120.4 %all-reduce.35 = bf16[2916,576]{0,1:T(8,128)(2,1)} all-reduce(f32[2916,576]{0,1:T(8,128)} %fusion.68), channel_id=8, replica_groups=mesh['dp'=4,'row'=4,'col'=2] {'row'}, use_global_device_ids=true, to_apply=%region_20.21.clone | all-reduce | flops 1679616 | bytes 10077696
  1658.8 35.4 %collective-permute-done.3 = bf16[729,1728]{1,0:T(8,128)(2,1)} collective-permute-done((bf16[729,1728]{1,0:T(8,128)(2,1)}, bf16[729,1728]{1,0:T(8,128)(2,1)}, u32[]{:S(2)}, u32[]{:S(2)}) %collective-permute-start.3) | collective-permute-done | bytes 2519456 | tf_op jit(solution)/shard_map/ppermute | solution.py:76
  1713.4 21.0 %collective-permute-done.4 = bf16[729,1728]{1,0:T(8,128)(2,1)} collective-permute-done((bf16[729,1728]{1,0:T(8,128)(2,1)}, bf16[729,1728]{1,0:T(8,128)(2,1)}, u32[]{:S(2)}, u32[]{:S(2)}) %collective-permute-start.4) | collective-permute-done | bytes 2519456 | tf_op jit(solution)/shard_map/ppermute | solution.py:76
  1734.5 101.1 %concatenate.15 = bf16[5832,1728]{1,0:T(8,128)(2,1)} concatenate(bf16[729,1728]{1,0:T(8,128)(2,1)} %collective-permute-done.4, bf16[729,1728]{1,0:T(8,128)(2,1)} %collective-permute-done.3, bf16[729,1728]{1,0:T(8,128)(2,1)} %copy.54, bf16[729,1728]{1,0:T(8,128)(2,1)} %collective-permute-done.5, bf16[729,1728]{1,0:T(8,128)(2,1)} %collective-permute-done.4, ...), dimensions={0} | concatenate | bytes 40310784 | tf_op jit(solution)/shard_map/jit(_roll_dynamic)/concatenate | solution.py:80
  1870.8 46.0 %all-reduce.34.cloned.1.call-done = bf16[288,3,576]{2,1,0:T(4,128)(2,1)} async-done(((bf16[288,3,576]{2,1,0:T(4,128)(2,1)}), bf16[288,3,576]{2,1,0:T(4,128)(2,1)}) %all-reduce.34.cloned.1.call-update) | async-done | bytes 995344
  1918.6 90.7 %all-reduce.32.cloned.1.call-done = f32[2916,288]{0,1:T(8,128)} async-done(((f32[2916,288]{0,1:T(8,128)}), f32[2916,288]{0,1:T(8,128)}) %all-reduce.32.cloned.1.call-update) | async-done | bytes 3359248
  2012.4 40.5 %all-reduce.14 = (f32[6,1152]{1,0:T(8,128)S(1)}, f32[2,1152]{1,0:T(2,128)S(1)}, f32[4304]{0:T(1024)S(1)}) all-reduce(f32[6,1152]{1,0:T(8,128)S(1)} %dynamic_update_slice.18, f32[2,1152]{1,0:T(2,128)S(1)} %dynamic_update_slice.19, f32[4304]{0:T(1024)S(1)} %dynamic_update_slice.20), channel_id=1, replica_groups=mesh['dp'=4,'row'=4,'col'=2] {'dp','row','col'}, use_global_device_ids=true, to_apply=%region_33.34 | all-reduce | flops 13520 | bytes 108160 | tf_op jit(solution)/shard_map/psum | solution.py:235
  (199 shorter events, 380.4 us)
Async XLA Ops:
  7.2 677.4 %copy-start = (bf16[288,2152]{1,0:T(8,128)(2,1)S(1)}, bf16[288,2152]{1,0:T(8,128)(2,1)}, u32[]{:S(2)}) copy-start(bf16[288,2152]{1,0:T(8,128)(2,1)} %param.19) | copy-start | bytes 3718660
  7.2 48.7 %all-gather.13.cloned.1.call-start = ((), (), s32[]{:S(2)}) async-start(), calls=%async_computation.4 | async-start | bytes 2654208 | tf_op jit(solution)/shard_map/all_gather | solution.py:43
  26.0 324.7 %all-gather.15.cloned.1.call-start = ((), (), s32[]{:S(2)}) async-start(), calls=%async_computation.5 | async-start | bytes 4423680 | tf_op jit(solution)/shard_map/all_gather | solution.py:95
  259.4 2.9 collective-permute-start.6
  316.8 64.9 %all-gather.21.cloned.1.call-start = ((), (), s32[]{:S(2)}) async-start(), calls=%async_computation.8 | async-start | bytes 2654208 | tf_op jit(solution)/shard_map/all_gather | solution.py:43
  317.5 120.6 %all-reduce.26.cloned.1.call-start = ((), (), s32[]{:S(2)}) async-start(), calls=%async_computation.10 | async-start | bytes 3391488
  369.7 305.1 %all-gather.17.cloned.1.call-start = ((), (), s32[]{:S(2)}) async-start(), calls=%async_computation.6 | async-start | bytes 2654208 | tf_op jit(solution)/shard_map/all_gather | solution.py:43
  454.1 825.4 %all-gather.19.cloned.1.call-start = ((), (), s32[]{:S(2)}) async-start(), calls=%async_computation.7 | async-start | bytes 16015360 | tf_op jit(solution)/shard_map/all_gather | solution.py:95
  673.3 246.5 %collective-permute-start.8 = (f32[21,2152]{1,0:T(8,128)S(1)}, f32[21,2152]{1,0:T(8,128)S(1)}, u32[]{:S(2)}, u32[]{:S(2)}) collective-permute-start(f32[21,2152]{1,0:T(8,128)S(1)} %slice.78), channel_id=1, source_target_pairs={{0,2},{2,4},{4,6},{1,3},{3,5},{5,7},{8,10},{10,12},{12,14},{9,11},... | collective-permute-start | bytes 542312
  918.5 18.8 collective-permute-start.7
  967.2 403.0 %all-reduce.30.cloned.1.call-start = ((), (), s32[]{:S(2)}) async-start(), calls=%async_computation.12 | async-start | bytes 6782976
  967.3 128.6 %collective-permute-start = (bf16[729,2152]{1,0:T(8,128)(2,1)}, bf16[729,2152]{1,0:T(8,128)(2,1)}, u32[]{:S(2)}, u32[]{:S(2)}) collective-permute-start(bf16[729,2152]{1,0:T(8,128)(2,1)} %get-tuple-element.93), channel_id=1, source_target_pairs={{0,2},{2,4},{4,6},{6,0},{1,3},{3,5},{5,7},{7,1},{8,10},{10,12},{12... | collective-permute-start | bytes 9412856 | tf_op jit(solution)/shard_map/ppermute | solution.py:76
  968.4 130.8 %collective-permute-start.2 = (bf16[729,2152]{1,0:T(8,128)(2,1)}, bf16[729,2152]{1,0:T(8,128)(2,1)}, u32[]{:S(2)}, u32[]{:S(2)}) collective-permute-start(bf16[729,2152]{1,0:T(8,128)(2,1)} %get-tuple-element.93), channel_id=1, source_target_pairs={{0,6},{2,0},{4,2},{6,4},{1,7},{3,1},{5,3},{7,5},{8,14},{10,8},{12,... | collective-permute-start | bytes 9412856 | tf_op jit(solution)/shard_map/ppermute | solution.py:78
  1095.9 46.4 %collective-permute-start.1 = (bf16[729,2152]{1,0:T(8,128)(2,1)}, bf16[729,2152]{1,0:T(8,128)(2,1)}, u32[]{:S(2)}, u32[]{:S(2)}) collective-permute-start(bf16[729,2152]{1,0:T(8,128)(2,1)} %collective-permute-done), channel_id=1, source_target_pairs={{0,2},{2,4},{4,6},{6,0},{1,3},{3,5},{5,7},{7,1},{8,10},{10,12},{12... | collective-permute-start | bytes 9412856 | tf_op jit(solution)/shard_map/ppermute | solution.py:76
  1279.5 147.3 %all-reduce.28.cloned.1.call-start = ((), (), s32[]{:S(2)}) async-start(), calls=%async_computation.11 | async-start | bytes 3391488
  1310.1 154.0 %all-gather.23.cloned.1.call-start = ((), (), s32[]{:S(2)}) async-start(), calls=%async_computation.9 | async-start | bytes 2654208 | tf_op jit(solution)/shard_map/all_gather | solution.py:43
  1434.5 428.9 %reduce-scatter.21.cloned.1.call-start = ((), (), s32[]{:S(2)}) async-start(), calls=%async_computation.15 | async-start | bytes 1566720
  1646.2 48.1 %collective-permute-start.3 = (bf16[729,1728]{1,0:T(8,128)(2,1)}, bf16[729,1728]{1,0:T(8,128)(2,1)}, u32[]{:S(2)}, u32[]{:S(2)}) collective-permute-start(bf16[729,1728]{1,0:T(8,128)(2,1)} %copy.54), channel_id=1, source_target_pairs={{0,2},{2,4},{4,6},{6,0},{1,3},{3,5},{5,7},{7,1},{8,10},{10,12},{12... | collective-permute-start | bytes 7558280 | tf_op jit(solution)/shard_map/ppermute | solution.py:76
  1657.5 207.7 %reduce-scatter.23.cloned.1.call-start = ((), (), s32[]{:S(2)}) async-start(), calls=%async_computation.16 | async-start | bytes 1566720
  1657.6 55.8 %collective-permute-start.5 = (bf16[729,1728]{1,0:T(8,128)(2,1)}, bf16[729,1728]{1,0:T(8,128)(2,1)}, u32[]{:S(2)}, u32[]{:S(2)}) collective-permute-start(bf16[729,1728]{1,0:T(8,128)(2,1)} %copy.54), channel_id=1, source_target_pairs={{0,6},{2,0},{4,2},{6,4},{1,7},{3,1},{5,3},{7,5},{8,14},{10,8},{12,... | collective-permute-start | bytes 7558280 | tf_op jit(solution)/shard_map/ppermute | solution.py:78
  1694.2 40.2 %collective-permute-start.4 = (bf16[729,1728]{1,0:T(8,128)(2,1)}, bf16[729,1728]{1,0:T(8,128)(2,1)}, u32[]{:S(2)}, u32[]{:S(2)}) collective-permute-start(bf16[729,1728]{1,0:T(8,128)(2,1)} %collective-permute-done.3), channel_id=1, source_target_pairs={{0,2},{2,4},{4,6},{6,0},{1,3},{3,5},{5,7},{7,1},{8,10},{10,12},{12... | collective-permute-start | bytes 7558280 | tf_op jit(solution)/shard_map/ppermute | solution.py:76
  1704.7 164.5 %reduce-scatter.19.cloned.1.call-start = ((), (), s32[]{:S(2)}) async-start(), calls=%async_computation.3 | async-start | bytes 552960 | tf_op jit(solution)/shard_map/reduce_scatter | solution.py:244
  1709.9 206.8 %all-reduce.34.cloned.1.call-start = ((), (), s32[]{:S(2)}) async-start(), calls=%async_computation.14 | async-start | bytes 2949120
  1851.4 158.0 %all-reduce.32.cloned.1.call-start = ((), (), s32[]{:S(2)}) async-start(), calls=%async_computation.13 | async-start | bytes 6782976
  (25 other events, 1198.3 us)
Sparse Core Ops, SparseCore 0:
  26.1 29.7 all-gather.12
  316.9 33.7 all-gather.14
  352.3 29.3 all-gather.20
  383.9 54.1 all-reduce.25
  454.2 29.0 all-gather.16
  967.4 146.6 all-gather.18
  1279.6 90.5 all-reduce.29
  1372.5 54.1 all-reduce.27
  1434.6 29.4 all-gather.22
  1657.7 29.9 reduce-scatter.20
  1704.8 30.5 reduce-scatter.22
  1738.1 20.1 reduce-scatter.18
  1851.5 65.1 all-reduce.33
  1918.9 90.4 all-reduce.31
